TPU v7x, 128 devices: a whole 4x4x4 slice. The times are simulated.
128 devices in a mesh: tok: 16 (over z, x_hi, core), req: 8 (over x_lo, y).
Axes of the slice: x: 4 (x_hi: 2, x_lo: 2; x = x_hi * 2 + x_lo), y: 4, z: 4, core: 2. Of those that a mesh axis runs over, the one named last changes fastest.
Arguments:
- query_rows: bfloat16 [8, 4096, 7168], P('req', 'tok'), may hold values from -16 to 16
- key_rows: bfloat16 [8, 4096, 7168], P('req', 'tok'), may hold values from -16 to 16
- value_rows: bfloat16 [8, 4096, 7168], P('req', 'tok'), may hold values from -6 to 6
- lengths: int32 [8, 6], P('req'), may hold values from 1 to 2048, 4096 in all within a row
- cache_blocks: bfloat16 [8, 128, 2, 32, 3584], P('req', 'tok'), may hold values from -6 to 6
- destinations: int32 [8, 128, 1], P('req', 'tok'), may hold values from 0 to 7; in each aligned block of 8 rows (0 to 7, 8 to 15, ..., all dimensions but the last counted through in order) at most 2 rows name the same one
Outputs:
- attended: bfloat16 [8, 4096, 7168], P('req', 'tok')
- moved_cache: bfloat16 [8, 8, 2, 2, 16, 32, 3584], P('req', None, None, None, None, 'tok')
Inputs may be any that keep to these rules, and one draw needn't show every extreme that they name: The 6 lengths of each span sum to 4096, and the longest of every span is exactly 2048. `destinations`: of the 8 rows of one device (aligned blocks of 8 rows), at most 2 name the same group, and in every draw some device names one group exactly 2 times.
All inputs are finite; a program needn't handle non-finite values.
Results may differ from a plain program's by a relative error of at most 0.0037.
Values may be sent and summed in bfloat16 or wider, within the bound.
A program may use at most 192 MiB of HBM per device.

v0:
```python
import jax
import jax.numpy as jnp
from jax import lax
from jax.sharding import PartitionSpec as P

HD = 224
CAP = 2


def segment_ids(lengths_row, span_length):
    ends = jnp.cumsum(lengths_row)
    positions = jnp.arange(span_length, dtype=jnp.int32)
    return jnp.sum((positions[:, None] >= ends[None, :]).astype(jnp.int32), axis=1)


def attend_item(query_all, key_all, value_all, segments):
    length = query_all.shape[0]
    heads_here = query_all.shape[1] // HD
    positions = jnp.arange(length, dtype=jnp.int32)
    block_rows = min(512, length)
    results = []
    for block_start in range(0, length, block_rows):
        block_end = block_start + block_rows
        visible = (segments[block_start:block_end, None] == segments[None, :block_end]) & (
            positions[block_start:block_end, None] >= positions[None, :block_end]
        )
        head_results = []
        for head in range(heads_here):
            low = head * HD
            high = low + HD
            query_block = query_all[block_start:block_end, low:high]
            key_block = key_all[:block_end, low:high]
            value_block = value_all[:block_end, low:high]
            scores = lax.dot_general(
                query_block, key_block, (((1,), (1,)), ((), ())), preferred_element_type=jnp.float32
            ) * HD ** (-0.5)
            scores = jnp.where(visible, scores, -1e30)
            row_max = jnp.max(scores, axis=1, keepdims=True)
            weights = jnp.where(visible, jnp.exp(scores - row_max), 0.0)
            row_total = jnp.sum(weights, axis=1, keepdims=True)
            summed = jnp.dot(
                weights.astype(jnp.bfloat16), value_block, preferred_element_type=jnp.float32
            )
            head_results.append((summed / row_total).astype(jnp.bfloat16))
        results.append(jnp.concatenate(head_results, axis=1))
    return jnp.concatenate(results, axis=0)


def attend_heads(parts, segments):
    query_part, key_part, value_part = parts
    length = query_part.shape[0]
    item_count = query_part.shape[2]
    outputs = [attend_item(query_part[:, 0, 0], key_part[:, 0, 0], value_part[:, 0, 0], segments)]
    return jnp.stack(outputs, axis=1).reshape(length, 1, item_count, query_part.shape[3])


def regroup_attend(query_rows, key_rows, value_rows, segments):
    tok_count = lax.axis_size("tok")
    token_rows = query_rows.shape[1]
    feature_width = query_rows.shape[2]
    group_width = feature_width // tok_count

    def by_group(rows_in):
        return rows_in[0].reshape(token_rows, tok_count, 1, group_width)

    mixed = attend_heads(
        (
            lax.all_to_all(by_group(query_rows), "tok", split_axis=1, concat_axis=0, tiled=True),
            lax.all_to_all(by_group(key_rows), "tok", split_axis=1, concat_axis=0, tiled=True),
            lax.all_to_all(by_group(value_rows), "tok", split_axis=1, concat_axis=0, tiled=True),
        ),
        segments=segments,
    )
    returned = lax.all_to_all(mixed, "tok", split_axis=0, concat_axis=1, tiled=True)
    return returned.reshape(1, token_rows, feature_width)


def relocate(cache_blocks, destinations):
    groups = lax.axis_size("req")
    tok_count = lax.axis_size("tok")
    targets = destinations[0, :, 0]
    block_count = targets.shape[0]
    positions = jnp.arange(block_count, dtype=jnp.int32)
    earlier = (targets[:, None] == targets[None, :]) & (positions[None, :] < positions[:, None])
    slot_rank = jnp.sum(earlier.astype(jnp.int32), axis=1)
    group_ids = jnp.arange(groups, dtype=jnp.int32)
    slot_ids = jnp.arange(CAP, dtype=jnp.int32)
    placing = (
        (targets[:, None, None] == group_ids[None, :, None])
        & (slot_rank[:, None, None] == slot_ids[None, None, :])
    ).astype(cache_blocks.dtype)
    local_blocks = cache_blocks[0]
    heads_all = local_blocks.shape[2]
    local_blocks = local_blocks.reshape(
        block_count, 2, tok_count, heads_all // tok_count, local_blocks.shape[3]
    )
    outgoing = jnp.einsum(
        "bdc,bjthy->dcjthy", placing, local_blocks, preferred_element_type=jnp.float32
    ).astype(jnp.bfloat16)
    arrived = lax.all_to_all(
        lax.all_to_all(outgoing, "tok", split_axis=3, concat_axis=3, tiled=True),
        "req",
        split_axis=0,
        concat_axis=0,
        tiled=True,
    )
    return arrived[None]


def on_device(query_rows, key_rows, value_rows, lengths, cache_blocks, destinations):
    span_length = query_rows.shape[1] * lax.axis_size("tok")
    segments = segment_ids(lengths[0], span_length)
    attended = regroup_attend(query_rows, key_rows, value_rows, segments)
    moved_cache = relocate(cache_blocks, destinations)
    return (attended, moved_cache)


def solution(mesh):
    return jax.shard_map(
        on_device,
        mesh=mesh,
        in_specs=(
            P("req", "tok", None),
            P("req", "tok", None),
            P("req", "tok", None),
            P("req", None),
            P("req", "tok", None, None, None),
            P("req", "tok", None),
        ),
        out_specs=(P("req", "tok", None), P("req", None, None, None, None, "tok", None)),
        check_vma=False,
    )
```

profile of v0, /device:TPU:1, one launch (start us, length us, event | category | flops | bytes accessed | tf_op | source)
XLA Modules:
  0.0 419.9 jit_solution(5922651007471697967)
XLA Ops:
  0.6 5.9 %copy.54 = bf16[1,256,7168]{1,2,0:T(8,128)(2,1)} copy(bf16[1,256,7168]{2,1,0:T(8,128)(2,1)} %param.7) | data formatting | bytes 7340032 | tf_op args[1]
  6.5 9.3 %all-to-all-start.1 = ((bf16[256,16,1,448]{0,3,2,1:T(8,128)(2,1)}), bf16[256,16,1,448]{0,3,2,1:T(8,128)(2,1)}, u32[]{:S(2)}, u32[]{:S(2)}) async-start(bf16[256,16,1,448]{0,3,2,1:T(8,128)(2,1)} %bitcast.60), calls=%async_computation.1 | async-start | bytes 7340032 | tf_op jit(solution)/shard_map/all_to_all | solution.py:69
  15.8 5.9 %copy.51 = bf16[1,256,7168]{1,2,0:T(8,128)(2,1)} copy(bf16[1,256,7168]{2,1,0:T(8,128)(2,1)} %param.6) | data formatting | bytes 7340032 | tf_op args[0]
  21.7 39.6 %all-to-all-done.1 = bf16[256,16,1,448]{0,3,2,1:T(8,128)(2,1)} async-done(((bf16[256,16,1,448]{0,3,2,1:T(8,128)(2,1)}), bf16[256,16,1,448]{0,3,2,1:T(8,128)(2,1)}, u32[]{:S(2)}, u32[]{:S(2)}) %all-to-all-start.1) | async-done | bytes 3670048 | tf_op jit(solution)/shard_map/all_to_all | solution.py:69
  61.3 5.2 %all-to-all-start = ((bf16[256,16,1,448]{0,3,2,1:T(8,128)(2,1)}), bf16[256,16,1,448]{0,3,2,1:T(8,128)(2,1)}, u32[]{:S(2)}, u32[]{:S(2)}) async-start(bf16[256,16,1,448]{0,3,2,1:T(8,128)(2,1)} %bitcast.59), calls=%async_computation | async-start | bytes 7340032 | tf_op jit(solution)/shard_map/all_to_all | solution.py:68
  66.5 5.9 %copy.57 = bf16[1,256,7168]{1,2,0:T(8,128)(2,1)} copy(bf16[1,256,7168]{2,1,0:T(8,128)(2,1)} %param.8) | data formatting | bytes 7340032 | tf_op args[2]
  72.4 5.9 %copy.69 = bf16[1,8,2,32,3584]{4,1,3,2,0:T(8,128)(2,1)} copy(bf16[1,8,2,32,3584]{4,3,2,1,0:T(8,128)(2,1)} %param.10) | data formatting | bytes 7340032 | tf_op jit(solution)/shard_map/reshape;squeeze | solution.py:94
  78.8 7.1 %convolution_convert_fusion = bf16[8,2,2,16,2,3584]{5,0,4,3,2,1:T(8,128)(2,1)} fusion(bf16[8,2,16,2,3584,1]{4,0,3,2,1,5:T(8,128)(2,1)} %bitcast.62, pred[8,2]{0,1:T(4,128)(4,1)S(1)} %iota_compare_fusion.4, pred[8,8]{0,1:T(8,128)(4,1)S(1)} %iota_compare_fusion.3), kind=kOutput, calls=%fused_computation.6 | convolution fusion | flops 62390400 | bytes 11010128 | tf_op jit(solution)/shard_map/bdc,bjthy->dcjthy/dot_general | solution.py:97
  86.0 26.1 %all-to-all-done = bf16[256,16,1,448]{0,3,2,1:T(8,128)(2,1)} async-done(((bf16[256,16,1,448]{0,3,2,1:T(8,128)(2,1)}), bf16[256,16,1,448]{0,3,2,1:T(8,128)(2,1)}, u32[]{:S(2)}, u32[]{:S(2)}) %all-to-all-start) | async-done | bytes 3670048 | tf_op jit(solution)/shard_map/all_to_all | solution.py:68
  112.0 5.8 %all-to-all-start.2 = ((bf16[256,16,1,448]{0,3,2,1:T(8,128)(2,1)}), bf16[256,16,1,448]{0,3,2,1:T(8,128)(2,1)}, u32[]{:S(2)}, u32[]{:S(2)}) async-start(bf16[256,16,1,448]{0,3,2,1:T(8,128)(2,1)} %bitcast.58), calls=%async_computation.2 | async-start | bytes 7340032 | tf_op jit(solution)/shard_map/all_to_all | solution.py:70
  118.0 6.7 %copy.64 = bf16[8,2,2,16,2,3584]{5,0,4,2,1,3:T(8,128)(2,1)} copy(bf16[8,2,2,16,2,3584]{5,0,4,3,2,1:T(8,128)(2,1)} %convolution_convert_fusion) | data formatting | bytes 14680064 | tf_op jit(solution)/shard_map/convert_element_type | solution.py:99
  127.2 3.8 copy.72
  144.8 4.5 %fusion.307 = (f32[512]{0:T(512)S(1)}, f32[512,3584]{1,0:T(8,128)}) fusion(bf16[4096,448]{0,1:T(8,128)(2,1)S(1)} %bitcast.78, bf16[4096,448]{0,1:T(8,128)(2,1)S(1)} %bitcast.94, s32[3584]{0:T(1024)S(1)} %iota_add_fusion, s32[512]{0:T(512)S(1)} %iota_add_fusion.7, s32[3584]{0:T(1024)S(1)} %bitcast.120, s32[512]{0:T(512)S(1)} %get-tuple-element.29), kind=kOutput, calls=%fused_computation.282 | convolution fusion | flops 833093120 | bytes 9213952 | tf_op jit(solution)/shard_map/dot_general | solution.py:34
  149.3 4.5 %fusion.308 = (f32[512]{0:T(512)S(1)}, f32[512,3584]{1,0:T(8,128)}) fusion(bf16[4096,448]{0,1:T(8,128)(2,1)S(1)} %bitcast.79, bf16[4096,448]{0,1:T(8,128)(2,1)S(1)} %bitcast.95, s32[3584]{0:T(1024)S(1)} %iota_add_fusion, s32[512]{0:T(512)S(1)} %iota_add_fusion.7, s32[3584]{0:T(1024)S(1)} %bitcast.121, s32[512]{0:T(512)S(1)} %get-tuple-element.29), kind=kOutput, calls=%fused_computation.283 | convolution fusion | flops 833093120 | bytes 9213952 | tf_op jit(solution)/shard_map/dot_general | solution.py:34
  153.8 9.5 %all-to-all-done.2 = bf16[256,16,1,448]{0,3,2,1:T(8,128)(2,1)} async-done(((bf16[256,16,1,448]{0,3,2,1:T(8,128)(2,1)}), bf16[256,16,1,448]{0,3,2,1:T(8,128)(2,1)}, u32[]{:S(2)}, u32[]{:S(2)}) %all-to-all-start.2) | async-done | bytes 3670048 | tf_op jit(solution)/shard_map/all_to_all | solution.py:70
  163.3 5.6 %all-to-all-start.4 = ((bf16[8,2,2,16,2,3584]{5,0,4,2,1,3:T(8,128)(2,1)}), bf16[8,2,2,16,2,3584]{5,0,4,2,1,3:T(8,128)(2,1)}, u32[]{:S(2)}, u32[]{:S(2)}) async-start(bf16[8,2,2,16,2,3584]{5,0,4,2,1,3:T(8,128)(2,1)} %copy.64), calls=%async_computation.4 | async-start | bytes 14680064 | tf_op jit(solution)/shard_map/all_to_all | solution.py:101
  218.3 4.5 %fusion.5 = (f32[512]{0:T(512)S(1)}, f32[512]{0:T(512)S(1)}) fusion(f32[512,3584]{1,0:T(8,128)S(1)} %bitcast.65, f32[512]{0:T(512)S(1)} %get-tuple-element.59, s32[3584]{0:T(1024)S(1)} %iota_add_fusion, s32[512]{0:T(512)S(1)} %iota_add_fusion.7, s32[3584]{0:T(1024)S(1)} %bitcast.122, s32[512]{0:T(512)S(1)} %get-tuple-element.29, ...), kind=kLoop, calls=%fused_computation.26 | loop fusion | flops 16514048 | bytes 14721024 | tf_op jit(solution)/shard_map/reduce_sum | solution.py:40
  231.6 4.6 %fusion.9 = (f32[512]{0:T(512)S(1)}, f32[512]{0:T(512)S(1)}, f32[512,4096]{1,0:T(8,128)S(1)}) fusion(f32[512,4096]{1,0:T(8,128)S(1)} %get-tuple-element.62, f32[512]{0:T(512)S(1)} %get-tuple-element.61, s32[512]{0:T(512)S(1)} %iota_add_fusion.6, s32[4096]{0:T(1024)S(1)} %convert_reduce_fusion, s32[512]{0:T(512)S(1)} %get-tuple-element.28, ...), kind=kOutput, calls=%fused_computation.30 | convolution fusion | flops 962591744 | bytes 18868224 | tf_op jit(solution)/shard_map/dot_general | solution.py:34
  246.9 6.2 %reduce = bf16[4096,448]{0,1:T(8,128)(2,1)} reduce(bf16[4096,1,1,448]{0,3,2,1:T(8,128)(2,1)} %bitcast.14, bf16[]{:T(256)} %broadcast.221), dimensions={1,2}, to_apply=%copy.60.reduce_sub_computation | reduce | bytes 7340034 | tf_op jit(solution)/shard_map/reshape;stack | solution.py:54
  253.1 6.3 %copy.77 = bf16[4096,448]{1,0:T(8,128)(2,1)} copy(bf16[4096,448]{0,1:T(8,128)(2,1)} %reduce) | data formatting | bytes 7340032
  259.4 12.3 %reshape.155 = bf16[16,2,57344]{2,1,0:T(2,128)(2,1)} reshape(bf16[4096,448]{1,0:T(8,128)(2,1)} %copy.77) | data formatting | bytes 7340032
  271.8 7.3 %all-to-all-start.3 = ((bf16[16,2,57344]{2,1,0:T(2,128)(2,1)}), bf16[16,2,57344]{2,1,0:T(2,128)(2,1)}, u32[]{:S(2)}, u32[]{:S(2)}) async-start(bf16[16,2,57344]{2,1,0:T(2,128)(2,1)} %reshape.155), calls=%async_computation.3 | async-start | bytes 7340032 | tf_op jit(solution)/shard_map/all_to_all | solution.py:74
  279.0 11.8 %copy.65 = bf16[8,2,2,16,2,3584]{5,4,3,2,1,0:T(2,128)(2,1)} copy(bf16[8,2,2,16,2,3584]{5,0,4,2,1,3:T(8,128)(2,1)} %all-to-all-done.4) | data formatting | bytes 14680064 | tf_op jit(solution)/shard_map/all_to_all | solution.py:101
  290.9 33.7 %all-to-all-done.3 = bf16[16,2,57344]{2,1,0:T(2,128)(2,1)} async-done(((bf16[16,2,57344]{2,1,0:T(2,128)(2,1)}), bf16[16,2,57344]{2,1,0:T(2,128)(2,1)}, u32[]{:S(2)}, u32[]{:S(2)}) %all-to-all-start.3) | async-done | bytes 3670048 | tf_op jit(solution)/shard_map/all_to_all | solution.py:74
  324.5 5.2 %all-to-all-start.5 = ((bf16[8,2,2,16,2,3584]{5,4,3,2,1,0:T(2,128)(2,1)}), bf16[8,2,2,16,2,3584]{5,4,3,2,1,0:T(2,128)(2,1)}, u32[]{:S(2)}, u32[]{:S(2)}) async-start(bf16[8,2,2,16,2,3584]{5,4,3,2,1,0:T(2,128)(2,1)} %copy.65), calls=%async_computation.5 | async-start | bytes 14680064 | tf_op jit(solution)/shard_map/all_to_all | solution.py:100
  329.7 13.2 %reshape.156 = bf16[4096,1,1,448]{3,2,1,0:T(2,128)(2,1)} reshape(bf16[16,2,57344]{2,1,0:T(2,128)(2,1)} %all-to-all-done.3) | data formatting | bytes 7340032
  342.9 6.6 %copy.70 = bf16[4096,1,1,448]{3,0,1,2:T(8,128)(2,1)} copy(bf16[4096,1,1,448]{3,2,1,0:T(2,128)(2,1)} %reshape.156) | data formatting | bytes 7340032
  349.5 7.7 %copy.68 = bf16[16,256,1,1,448]{1,0,4,3,2:T(8,128)(2,1)} copy(bf16[16,256,1,1,448]{4,1,0,3,2:T(8,128)(2,1)} %bitcast.57) | data formatting | bytes 7340032 | tf_op jit(solution)/shard_map/all_to_all | solution.py:74
  357.2 5.1 %copy.62 = bf16[256,16,1,1,448]{0,4,1,3,2:T(8,128)(2,1)} copy(bf16[256,16,1,1,448]{0,1,4,3,2:T(8,128)(2,1)} %bitcast.63) | data formatting | bytes 7340032 | tf_op jit(solution)/shard_map/all_to_all | solution.py:74
  362.3 5.9 %copy.66 = bf16[1,256,7168]{2,1,0:T(8,128)(2,1)} copy(bf16[1,256,7168]{1,2,0:T(8,128)(2,1)} %bitcast.61) | data formatting | bytes 7340032
  368.2 43.8 %all-to-all-done.5 = bf16[8,2,2,16,2,3584]{5,4,3,2,1,0:T(2,128)(2,1)} async-done(((bf16[8,2,2,16,2,3584]{5,4,3,2,1,0:T(2,128)(2,1)}), bf16[8,2,2,16,2,3584]{5,4,3,2,1,0:T(2,128)(2,1)}, u32[]{:S(2)}, u32[]{:S(2)}) %all-to-all-start.5) | async-done | bytes 7340064 | tf_op jit(solution)/shard_map/all_to_all | solution.py:100
  412.1 7.6 %copy.86 = bf16[1,8,2,2,16,2,3584]{6,5,4,3,2,1,0:T(2,128)(2,1)} copy(bf16[1,8,2,2,16,2,3584]{6,5,4,3,2,1,0:T(2,128)(2,1)} %bitcast.22) | data formatting | bytes 14680064
  (111 shorter events, 85.2 us)
Async XLA Ops:
  6.5 54.8 %all-to-all-start.1 = ((bf16[256,16,1,448]{0,3,2,1:T(8,128)(2,1)}), bf16[256,16,1,448]{0,3,2,1:T(8,128)(2,1)}, u32[]{:S(2)}, u32[]{:S(2)}) async-start(bf16[256,16,1,448]{0,3,2,1:T(8,128)(2,1)} %bitcast.60), calls=%async_computation.1 | async-start | bytes 7340032 | tf_op jit(solution)/shard_map/all_to_all | solution.py:69
  61.3 50.7 %all-to-all-start = ((bf16[256,16,1,448]{0,3,2,1:T(8,128)(2,1)}), bf16[256,16,1,448]{0,3,2,1:T(8,128)(2,1)}, u32[]{:S(2)}, u32[]{:S(2)}) async-start(bf16[256,16,1,448]{0,3,2,1:T(8,128)(2,1)} %bitcast.59), calls=%async_computation | async-start | bytes 7340032 | tf_op jit(solution)/shard_map/all_to_all | solution.py:68
  72.4 5.9 %copy-start.7 = (s32[1,6]{1,0:T(1,128)S(1)}, s32[1,6]{1,0:T(1,128)}, u32[]{:S(2)}) copy-start(s32[1,6]{1,0:T(1,128)} %param.9) | copy-start | bytes 76
  72.4 6.2 %copy-start.8 = (s32[1,8,1]{1,2,0:T(1,128)S(1)}, s32[1,8,1]{1,2,0:T(1,128)}, u32[]{:S(2)}) copy-start(s32[1,8,1]{1,2,0:T(1,128)} %param.11) | copy-start | bytes 100
  112.0 51.3 %all-to-all-start.2 = ((bf16[256,16,1,448]{0,3,2,1:T(8,128)(2,1)}), bf16[256,16,1,448]{0,3,2,1:T(8,128)(2,1)}, u32[]{:S(2)}, u32[]{:S(2)}) async-start(bf16[256,16,1,448]{0,3,2,1:T(8,128)(2,1)} %bitcast.58), calls=%async_computation.2 | async-start | bytes 7340032 | tf_op jit(solution)/shard_map/all_to_all | solution.py:70
  127.2 22.1 %copy-start = (bf16[56,8,16,256]{3,1,2,0:T(8,128)(2,1)}, bf16[56,8,16,256]{3,1,2,0:T(8,128)(2,1)S(1)}, u32[]{:S(2)}) copy-start(bf16[56,8,16,256]{3,1,2,0:T(8,128)(2,1)S(1)} %copy.73) | copy-start | bytes 11010052
  131.0 18.2 %copy-start.2 = (bf16[56,8,16,256]{3,1,2,0:T(8,128)(2,1)}, bf16[56,8,16,256]{3,1,2,0:T(8,128)(2,1)S(1)}, u32[]{:S(2)}) copy-start(bf16[56,8,16,256]{3,1,2,0:T(8,128)(2,1)S(1)} %copy.72) | copy-start | bytes 11010052
  163.3 108.5 %all-to-all-start.4 = ((bf16[8,2,2,16,2,3584]{5,0,4,2,1,3:T(8,128)(2,1)}), bf16[8,2,2,16,2,3584]{5,0,4,2,1,3:T(8,128)(2,1)}, u32[]{:S(2)}, u32[]{:S(2)}) async-start(bf16[8,2,2,16,2,3584]{5,0,4,2,1,3:T(8,128)(2,1)} %copy.64), calls=%async_computation.4 | async-start | bytes 14680064 | tf_op jit(solution)/shard_map/all_to_all | solution.py:101
  169.0 2.7 copy-start.5
  169.0 2.7 copy-start.6
  172.1 2.0 copy-start.1
  172.1 3.2 copy-start.3
  179.2 1.9 copy-start.4
  191.2 3.2 slice-start.4
  191.2 3.5 slice-start.6
  192.7 2.3 slice-start.5
  192.8 2.6 slice-start.7
  212.1 6.2 %slice-start = ((s8[7340032]{0:T(1024)(128)(4,1)}), s8[4194304]{0:T(1024)(128)(4,1)S(1)}, s32[]{:S(2)}) async-start(s8[7340032]{0:T(1024)(128)(4,1)} %bitcast.64), calls=%async_computation.6 | async-start | bytes 8388608
  212.1 6.2 %slice-start.2 = ((s8[7340032]{0:T(1024)(128)(4,1)}), s8[4194304]{0:T(1024)(128)(4,1)S(1)}, s32[]{:S(2)}) async-start(s8[7340032]{0:T(1024)(128)(4,1)} %bitcast.66), calls=%async_computation.8 | async-start | bytes 8388608
  212.1 6.2 %slice-start.1 = ((s8[7340032]{0:T(1024)(128)(4,1)}), s8[3145728]{0:T(1024)(128)(4,1)S(1)}, s32[]{:S(2)}) async-start(s8[7340032]{0:T(1024)(128)(4,1)} %bitcast.64), calls=%async_computation.7 | async-start | bytes 6291456
  212.1 6.2 %slice-start.3 = ((s8[7340032]{0:T(1024)(128)(4,1)}), s8[3145728]{0:T(1024)(128)(4,1)S(1)}, s32[]{:S(2)}) async-start(s8[7340032]{0:T(1024)(128)(4,1)} %bitcast.66), calls=%async_computation.9 | async-start | bytes 6291456
  271.8 52.8 %all-to-all-start.3 = ((bf16[16,2,57344]{2,1,0:T(2,128)(2,1)}), bf16[16,2,57344]{2,1,0:T(2,128)(2,1)}, u32[]{:S(2)}, u32[]{:S(2)}) async-start(bf16[16,2,57344]{2,1,0:T(2,128)(2,1)} %reshape.155), calls=%async_computation.3 | async-start | bytes 7340032 | tf_op jit(solution)/shard_map/all_to_all | solution.py:74
  324.5 87.5 %all-to-all-start.5 = ((bf16[8,2,2,16,2,3584]{5,4,3,2,1,0:T(2,128)(2,1)}), bf16[8,2,2,16,2,3584]{5,4,3,2,1,0:T(2,128)(2,1)}, u32[]{:S(2)}, u32[]{:S(2)}) async-start(bf16[8,2,2,16,2,3584]{5,4,3,2,1,0:T(2,128)(2,1)} %copy.65), calls=%async_computation.5 | async-start | bytes 14680064 | tf_op jit(solution)/shard_map/all_to_all | solution.py:100
where the time goes:
time: 427 us; the launch traced here: 420 us
  waiting for transfers between devices  153 us (36%)
  local copies, waits for them, and re-layouts  121 us (28%)
  matrix products  74.7 us (17%)
  starting transfers between devices  38.4 us (9%)
  other arithmetic  32.1 us (8%)
    unnamed x46, local copies, waits for them, and re-layouts  82.9 us
    all_to_all x1, waiting for transfers between devices, relocate(): lax.all_to_all(lax.all_to_all(outgoing, 'tok', split_axis=3, concat_axis=...  43.8 us
    dot_general x16, matrix products, attend_item(): lax.dot_general(query_block, key_block, (((1,), (1,)), ((), ())), preferr...  41.7 us
    all_to_all x1, waiting for transfers between devices, regroup_attend(): lax.all_to_all(by_group(key_rows), 'tok', split_axis=1, concat_axis=0, ti...  39.6 us
    all_to_all x1, waiting for transfers between devices, regroup_attend(): lax.all_to_all(mixed, 'tok', split_axis=0, concat_axis=1, tiled=True)  33.7 us
    all_to_all x1, waiting for transfers between devices, regroup_attend(): lax.all_to_all(by_group(query_rows), 'tok', split_axis=1, concat_axis=0,...  26.1 us
    dot_general x16, matrix products, attend_item(): jnp.dot(weights.astype(jnp.bfloat16), value_block, preferred_element_type...  25.8 us
    reduce_sum x8, other arithmetic, attend_item(): row_total = jnp.sum(weights, axis=1, keepdims=True)  19.1 us
  transfers between devices with their start and end apart: 6, of which 5 were waited for; matrix products, arithmetic and copies ran while one was open for 50% of the time, Pallas kernels for 0%

commit v1 on v0

--- a/solution.py
+++ b/solution.py
@@ -71,7 +71,10 @@
         ),
         segments=segments,
     )
-    returned = lax.all_to_all(mixed, "tok", split_axis=0, concat_axis=1, tiled=True)
+    size = lax.axis_size("tok")
+    blocks = jnp.stack(jnp.split(mixed, size, axis=0), axis=0)
+    blocks = lax.all_to_all(blocks, "tok", split_axis=0, concat_axis=0)
+    returned = jnp.concatenate(blocks, axis=1)
     return returned.reshape(1, token_rows, feature_width)
 
 

time: 427 us -> 409 us (0.958)
  local copies, waits for them, and re-layouts: 121 us -> 64.7 us
  waiting for transfers between devices: 153 us -> 187 us
  other arithmetic: 32.1 us -> 38.1 us
    unnamed x46, local copies, waits for them, and re-layouts: 82.9 us -> 45.2 us
    all_to_all x1, waiting for transfers between devices: 43.8 us -> 76.7 us  [relocate(): lax.all_to_all(lax.all_to_all(outgoing, 'tok', split_axis=3, concat_axis=...]
    all_to_all x2 -> x0, local copies, waits for them, and re-layouts: 12.9 us -> none  [regroup_attend(): lax.all_to_all(mixed, 'tok', split_axis=0, concat_axis=1, tiled=True)]
    reduce_sum x8, other arithmetic: 19.1 us -> 26.3 us  [attend_item(): row_total = jnp.sum(weights, axis=1, keepdims=True)]
    another operation x2, other arithmetic: 6.34 us -> 0.89 us  [the longest x1 0.71 us: regroup_attend(): blocks = jnp.stack(jnp.split(mixed, size, axis=0), axis=0)]
    dot_general x1, matrix products: 7.13 us -> 2.04 us  [relocate(): jnp.einsum('bdc,bjthy->dcjthy', placing, local_blocks, preferred_element_...]
    unnamed x11 -> x20, other arithmetic: 5.59 us -> 10.6 us
  transfers between devices with their start and end apart: 6 -> 6, of which waited for: 5 -> 5; matrix products, arithmetic and copies ran while one was open for 50% -> 39% of each run, Pallas kernels for 0% -> 0%
where the time goes in v1:
time: 409 us; the launch traced here: 403 us
  waiting for transfers between devices  187 us (46%)
  matrix products  73.6 us (18%)
  local copies, waits for them, and re-layouts  64.7 us (16%)
  starting transfers between devices  38.1 us (9%)
  other arithmetic  38.1 us (9%)
    all_to_all x1, waiting for transfers between devices, relocate(): lax.all_to_all(lax.all_to_all(outgoing, 'tok', split_axis=3, concat_axis=...  76.7 us
    dot_general x16, matrix products, attend_item(): lax.dot_general(query_block, key_block, (((1,), (1,)), ((), ())), preferr...  45.6 us
    unnamed x46, local copies, waits for them, and re-layouts  45.2 us
    all_to_all x1, waiting for transfers between devices, regroup_attend(): lax.all_to_all(by_group(key_rows), 'tok', split_axis=1, concat_axis=0, ti...  39.6 us
    all_to_all x1, waiting for transfers between devices, regroup_attend(): blocks = lax.all_to_all(blocks, 'tok', split_axis=0, concat_axis=0)  33.7 us
    reduce_sum x8, other arithmetic, attend_item(): row_total = jnp.sum(weights, axis=1, keepdims=True)  26.3 us
    dot_general x16, matrix products, attend_item(): jnp.dot(weights.astype(jnp.bfloat16), value_block, preferred_element_type...  25.9 us
    all_to_all x1, waiting for transfers between devices, regroup_attend(): lax.all_to_all(by_group(query_rows), 'tok', split_axis=1, concat_axis=0,...  24.9 us
  transfers between devices with their start and end apart: 6, of which 5 were waited for; matrix products, arithmetic and copies ran while one was open for 39% of the time, Pallas kernels for 0%

profile of v1, /device:TPU:1, one launch (start us, length us, event | category | flops | bytes accessed | tf_op | source)
XLA Modules:
  0.0 403.2 jit_solution(3388631596393671384)
XLA Ops:
  0.6 5.9 %copy.36 = bf16[1,256,7168]{1,2,0:T(8,128)(2,1)} copy(bf16[1,256,7168]{2,1,0:T(8,128)(2,1)} %param.7) | data formatting | bytes 7340032 | tf_op args[1]
  6.5 9.3 %all-to-all-start.1 = ((bf16[256,16,1,448]{0,3,2,1:T(8,128)(2,1)}), bf16[256,16,1,448]{0,3,2,1:T(8,128)(2,1)}, u32[]{:S(2)}, u32[]{:S(2)}) async-start(bf16[256,16,1,448]{0,3,2,1:T(8,128)(2,1)} %bitcast.140), calls=%async_computation.1 | async-start | bytes 7340032 | tf_op jit(solution)/shard_map/all_to_all | solution.py:69
  15.8 5.9 %copy.33 = bf16[1,256,7168]{1,2,0:T(8,128)(2,1)} copy(bf16[1,256,7168]{2,1,0:T(8,128)(2,1)} %param.6) | data formatting | bytes 7340032 | tf_op args[0]
  21.7 39.6 %all-to-all-done.1 = bf16[256,16,1,448]{0,3,2,1:T(8,128)(2,1)} async-done(((bf16[256,16,1,448]{0,3,2,1:T(8,128)(2,1)}), bf16[256,16,1,448]{0,3,2,1:T(8,128)(2,1)}, u32[]{:S(2)}, u32[]{:S(2)}) %all-to-all-start.1) | async-done | bytes 3670048 | tf_op jit(solution)/shard_map/all_to_all | solution.py:69
  61.3 5.3 %all-to-all-start = ((bf16[256,16,1,448]{0,3,2,1:T(8,128)(2,1)}), bf16[256,16,1,448]{0,3,2,1:T(8,128)(2,1)}, u32[]{:S(2)}, u32[]{:S(2)}) async-start(bf16[256,16,1,448]{0,3,2,1:T(8,128)(2,1)} %bitcast.139), calls=%async_computation | async-start | bytes 7340032 | tf_op jit(solution)/shard_map/all_to_all | solution.py:68
  67.0 5.9 %copy.39 = bf16[1,256,7168]{1,2,0:T(8,128)(2,1)} copy(bf16[1,256,7168]{2,1,0:T(8,128)(2,1)} %param.8) | data formatting | bytes 7340032 | tf_op args[2]
  72.9 4.1 %copy.47 = bf16[1,8,2,32,3584]{4,1,3,2,0:T(8,128)(2,1)S(1)} copy(bf16[1,8,2,32,3584]{4,3,2,1,0:T(8,128)(2,1)} %param.10) | data formatting | bytes 7340032 | tf_op jit(solution)/shard_map/reshape;squeeze | solution.py:97
  79.2 3.6 copy.43
  82.9 4.4 %copy.50 = bf16[56,8,16,256]{3,1,2,0:T(8,128)(2,1)} copy(bf16[56,8,16,256]{3,1,0,2:T(8,128)(2,1)} %bitcast.112) | data formatting | bytes 7340032
  87.3 24.9 %all-to-all-done = bf16[256,16,1,448]{0,3,2,1:T(8,128)(2,1)} async-done(((bf16[256,16,1,448]{0,3,2,1:T(8,128)(2,1)}), bf16[256,16,1,448]{0,3,2,1:T(8,128)(2,1)}, u32[]{:S(2)}, u32[]{:S(2)}) %all-to-all-start) | async-done | bytes 3670048 | tf_op jit(solution)/shard_map/all_to_all | solution.py:68
  112.2 5.5 %all-to-all-start.2 = ((bf16[256,16,1,448]{0,3,2,1:T(8,128)(2,1)}), bf16[256,16,1,448]{0,3,2,1:T(8,128)(2,1)}, u32[]{:S(2)}, u32[]{:S(2)}) async-start(bf16[256,16,1,448]{0,3,2,1:T(8,128)(2,1)} %bitcast.138), calls=%async_computation.2 | async-start | bytes 7340032 | tf_op jit(solution)/shard_map/all_to_all | solution.py:70
  131.2 3.7 fusion.85
  134.9 3.4 fusion.345
  138.3 3.5 fusion.346
  141.8 4.5 %fusion.347 = (f32[512]{0:T(512)S(1)}, f32[512,3584]{1,0:T(8,128)}) fusion(bf16[4096,448]{0,1:T(8,128)(2,1)S(1)} %bitcast.131, bf16[4096,448]{0,1:T(8,128)(2,1)S(1)} %bitcast.155, s32[3584]{0:T(1024)S(1)} %iota_add_fusion, s32[512]{0:T(512)S(1)} %iota_add_fusion.7, s32[3584]{0:T(1024)S(1)} %bitcast.182, s32[512]{0:T(512)S(1)} %get-tuple-element.35), kind=kOutput, calls=%fused_computation.338 | convolution fusion | flops 833093120 | bytes 9213952 | tf_op jit(solution)/shard_map/dot_general | solution.py:34
  146.3 4.5 %fusion.348 = (f32[512]{0:T(512)S(1)}, f32[512,3584]{1,0:T(8,128)}) fusion(bf16[4096,448]{0,1:T(8,128)(2,1)S(1)} %bitcast.132, bf16[4096,448]{0,1:T(8,128)(2,1)S(1)} %bitcast.156, s32[3584]{0:T(1024)S(1)} %iota_add_fusion, s32[512]{0:T(512)S(1)} %iota_add_fusion.7, s32[3584]{0:T(1024)S(1)} %bitcast.183, s32[512]{0:T(512)S(1)} %get-tuple-element.35), kind=kOutput, calls=%fused_computation.339 | convolution fusion | flops 833093120 | bytes 9213952 | tf_op jit(solution)/shard_map/dot_general | solution.py:34
  150.8 12.4 %all-to-all-done.2 = bf16[256,16,1,448]{0,3,2,1:T(8,128)(2,1)} async-done(((bf16[256,16,1,448]{0,3,2,1:T(8,128)(2,1)}), bf16[256,16,1,448]{0,3,2,1:T(8,128)(2,1)}, u32[]{:S(2)}, u32[]{:S(2)}) %all-to-all-start.2) | async-done | bytes 3670048 | tf_op jit(solution)/shard_map/all_to_all | solution.py:70
  163.1 5.9 %all-to-all-start.4 = ((bf16[8,2,2,16,2,3584]{5,0,4,2,1,3:T(8,128)(2,1)}), bf16[8,2,2,16,2,3584]{5,0,4,2,1,3:T(8,128)(2,1)}, u32[]{:S(2)}, u32[]{:S(2)}) async-start(bf16[8,2,2,16,2,3584]{5,0,4,2,1,3:T(8,128)(2,1)} %copy.43), calls=%async_computation.4 | async-start | bytes 14680064 | tf_op jit(solution)/shard_map/all_to_all | solution.py:104
  190.8 3.4 fusion.51
  198.8 3.2 fusion.29
  205.3 3.8 fusion.4
  209.1 4.8 %fusion.33 = (f32[512]{0:T(512)S(1)}, f32[512]{0:T(512)S(1)}) fusion(f32[512,3072]{1,0:T(8,128)S(1)} %get-tuple-element.56, f32[512]{0:T(512)S(1)} %get-tuple-element.14, s32[3072]{0:T(1024)S(1)} %iota_add_fusion.1, s32[512]{0:T(512)S(1)} %iota_add_fusion.8, s32[3072]{0:T(1024)S(1)} %slice.378, s32[512]{0:T(512)S(1)} %get-tuple-element.36, ...), kind=kLoop, calls=%fused_computation.55 | loop fusion | flops 20446208 | bytes 12619776 | tf_op jit(solution)/shard_map/reduce_sum | solution.py:40
  221.3 4.3 %fusion.7 = (f32[512]{0:T(512)S(1)}, f32[512]{0:T(512)S(1)}) fusion(f32[512,3584]{1,0:T(8,128)S(1)} %bitcast.143, f32[512]{0:T(512)S(1)} %get-tuple-element.59, s32[3584]{0:T(1024)S(1)} %iota_add_fusion, s32[512]{0:T(512)S(1)} %iota_add_fusion.7, s32[3584]{0:T(1024)S(1)} %bitcast.184, s32[512]{0:T(512)S(1)} %get-tuple-element.35, ...), kind=kLoop, calls=%fused_computation.28 | loop fusion | flops 16514048 | bytes 14721024 | tf_op jit(solution)/shard_map/reduce_sum | solution.py:40
  236.5 4.7 %fusion.2 = (f32[512]{0:T(512)S(1)}, f32[512]{0:T(512)S(1)}, f32[512,4096]{1,0:T(8,128)S(1)}) fusion(s32[512]{0:T(512)S(1)} %iota_add_fusion.6, s32[4096]{0:T(1024)S(1)} %convert_reduce_fusion, s32[512]{0:T(512)S(1)} %get-tuple-element.34, f32[512,4096]{1,0:T(8,128)S(1)} %fusion.67, bf16[4096,448]{0,1:T(8,128)(2,1)S(1)} %bitcast.137, ...), kind=kOutput, calls=%fused_computation.8 | convolution fusion | flops 958397440 | bytes 18866176 | tf_op jit(solution)/shard_map/dot_general | solution.py:34
  241.2 6.4 %fusion.11 = (f32[512]{0:T(512)S(1)}, f32[512]{0:T(512)S(1)}) fusion(f32[512,4096]{1,0:T(8,128)S(1)} %get-tuple-element.61, f32[512]{0:T(512)S(1)} %get-tuple-element.20, s32[512]{0:T(512)S(1)} %iota_add_fusion.6, s32[4096]{0:T(1024)S(1)} %convert_reduce_fusion, s32[512]{0:T(512)S(1)} %get-tuple-element.34, f32[512]{0:T(512)S(1)} %get-tuple-element.21, ...), kind=kLoop, calls=%fused_computation.32 | loop fusion | flops 27261952 | bytes 16805888 | tf_op jit(solution)/shard_map/reduce_sum | solution.py:40
  255.0 7.3 %all-to-all-start.3 = ((bf16[16,256,1,1,448]{1,4,3,2,0:T(8,128)(2,1)}), bf16[16,256,1,1,448]{1,4,3,2,0:T(8,128)(2,1)}, u32[]{:S(2)}, u32[]{:S(2)}) async-start(bf16[16,256,1,1,448]{1,4,3,2,0:T(8,128)(2,1)} %fusion.266), calls=%async_computation.3 | async-start | bytes 7340032 | tf_op jit(solution)/shard_map/all_to_all | solution.py:76
  262.2 11.8 %copy.44 = bf16[8,2,2,16,2,3584]{5,4,3,2,1,0:T(2,128)(2,1)} copy(bf16[8,2,2,16,2,3584]{5,0,4,2,1,3:T(8,128)(2,1)} %all-to-all-done.4) | data formatting | bytes 14680064 | tf_op jit(solution)/shard_map/all_to_all | solution.py:104
  274.1 33.7 %all-to-all-done.3 = bf16[16,256,1,1,448]{1,4,3,2,0:T(8,128)(2,1)} async-done(((bf16[16,256,1,1,448]{1,4,3,2,0:T(8,128)(2,1)}), bf16[16,256,1,1,448]{1,4,3,2,0:T(8,128)(2,1)}, u32[]{:S(2)}, u32[]{:S(2)}) %all-to-all-start.3) | async-done | bytes 3670048 | tf_op jit(solution)/shard_map/all_to_all | solution.py:76
  307.7 4.8 %all-to-all-start.5 = ((bf16[8,2,2,16,2,3584]{5,4,3,2,1,0:T(2,128)(2,1)}), bf16[8,2,2,16,2,3584]{5,4,3,2,1,0:T(2,128)(2,1)}, u32[]{:S(2)}, u32[]{:S(2)}) async-start(bf16[8,2,2,16,2,3584]{5,4,3,2,1,0:T(2,128)(2,1)} %copy.44), calls=%async_computation.5 | async-start | bytes 14680064 | tf_op jit(solution)/shard_map/all_to_all | solution.py:103
  312.6 5.9 %copy.45 = bf16[1,256,7168]{2,1,0:T(8,128)(2,1)} copy(bf16[1,256,7168]{1,2,0:T(8,128)(2,1)} %bitcast.31) | data formatting | bytes 7340032
  318.5 76.7 %all-to-all-done.5 = bf16[8,2,2,16,2,3584]{5,4,3,2,1,0:T(2,128)(2,1)} async-done(((bf16[8,2,2,16,2,3584]{5,4,3,2,1,0:T(2,128)(2,1)}), bf16[8,2,2,16,2,3584]{5,4,3,2,1,0:T(2,128)(2,1)}, u32[]{:S(2)}, u32[]{:S(2)}) %all-to-all-start.5) | async-done | bytes 7340064 | tf_op jit(solution)/shard_map/all_to_all | solution.py:103
  395.2 7.6 %copy.70 = bf16[1,8,2,2,16,2,3584]{6,5,4,3,2,1,0:T(2,128)(2,1)} copy(bf16[1,8,2,2,16,2,3584]{6,5,4,3,2,1,0:T(2,128)(2,1)} %bitcast.37) | data formatting | bytes 14680064
  (116 shorter events, 71.1 us)
Async XLA Ops:
  6.5 54.8 %all-to-all-start.1 = ((bf16[256,16,1,448]{0,3,2,1:T(8,128)(2,1)}), bf16[256,16,1,448]{0,3,2,1:T(8,128)(2,1)}, u32[]{:S(2)}, u32[]{:S(2)}) async-start(bf16[256,16,1,448]{0,3,2,1:T(8,128)(2,1)} %bitcast.140), calls=%async_computation.1 | async-start | bytes 7340032 | tf_op jit(solution)/shard_map/all_to_all | solution.py:69
  61.3 5.3 %copy-start.7 = (s32[1,6]{1,0:T(1,128)S(1)}, s32[1,6]{1,0:T(1,128)}, u32[]{:S(2)}) copy-start(s32[1,6]{1,0:T(1,128)} %param.9) | copy-start | bytes 76
  61.3 50.9 %all-to-all-start = ((bf16[256,16,1,448]{0,3,2,1:T(8,128)(2,1)}), bf16[256,16,1,448]{0,3,2,1:T(8,128)(2,1)}, u32[]{:S(2)}, u32[]{:S(2)}) async-start(bf16[256,16,1,448]{0,3,2,1:T(8,128)(2,1)} %bitcast.139), calls=%async_computation | async-start | bytes 7340032 | tf_op jit(solution)/shard_map/all_to_all | solution.py:68
  72.9 4.1 %copy-start.8 = (s32[1,8,1]{1,2,0:T(1,128)S(1)}, s32[1,8,1]{1,2,0:T(1,128)}, u32[]{:S(2)}) copy-start(s32[1,8,1]{1,2,0:T(1,128)} %param.11) | copy-start | bytes 100
  112.2 50.9 %all-to-all-start.2 = ((bf16[256,16,1,448]{0,3,2,1:T(8,128)(2,1)}), bf16[256,16,1,448]{0,3,2,1:T(8,128)(2,1)}, u32[]{:S(2)}, u32[]{:S(2)}) async-start(bf16[256,16,1,448]{0,3,2,1:T(8,128)(2,1)} %bitcast.138), calls=%async_computation.2 | async-start | bytes 7340032 | tf_op jit(solution)/shard_map/all_to_all | solution.py:70
  117.7 3.1 copy-start
  120.4 25.9 %copy-start.3 = (bf16[56,8,16,256]{3,1,2,0:T(8,128)(2,1)}, bf16[56,8,16,256]{3,1,2,0:T(8,128)(2,1)S(1)}, u32[]{:S(2)}) copy-start(bf16[56,8,16,256]{3,1,2,0:T(8,128)(2,1)S(1)} %copy.49) | copy-start | bytes 11010052
  163.1 91.8 %all-to-all-start.4 = ((bf16[8,2,2,16,2,3584]{5,0,4,2,1,3:T(8,128)(2,1)}), bf16[8,2,2,16,2,3584]{5,0,4,2,1,3:T(8,128)(2,1)}, u32[]{:S(2)}, u32[]{:S(2)}) async-start(bf16[8,2,2,16,2,3584]{5,0,4,2,1,3:T(8,128)(2,1)} %copy.43), calls=%async_computation.4 | async-start | bytes 14680064 | tf_op jit(solution)/shard_map/all_to_all | solution.py:104
  169.0 2.6 copy-start.6
  172.1 2.3 copy-start.1
  179.1 2.4 copy-start.4
  179.1 3.0 copy-start.5
  185.3 2.5 copy-start.2
  194.2 4.6 %slice-start.6 = ((s8[5242880]{0:T(1024)(128)(4,1)}), s8[1048576]{0:T(1024)(128)(4,1)S(1)}, s32[]{:S(2)}) async-start(s8[5242880]{0:T(1024)(128)(4,1)} %bitcast.162), calls=%async_computation.12 | async-start | bytes 2097152
  194.2 4.6 %slice-start.8 = ((s8[5242880]{0:T(1024)(128)(4,1)}), s8[4194304]{0:T(1024)(128)(4,1)S(1)}, s32[]{:S(2)}) async-start(s8[5242880]{0:T(1024)(128)(4,1)} %bitcast.164), calls=%async_computation.14 | async-start | bytes 8388608
  195.8 3.0 slice-start.7
  195.8 3.0 slice-start.9
  202.0 3.3 slice-start
  203.6 1.7 slice-start.1
  216.1 2.2 slice-start.2
  216.1 3.5 slice-start.4
  216.1 4.3 %slice-start.3 = ((s8[7340032]{0:T(1024)(128)(4,1)}), s8[3145728]{0:T(1024)(128)(4,1)S(1)}, s32[]{:S(2)}) async-start(s8[7340032]{0:T(1024)(128)(4,1)} %bitcast.142), calls=%async_computation.9 | async-start | bytes 6291456
  216.1 5.2 %slice-start.5 = ((s8[7340032]{0:T(1024)(128)(4,1)}), s8[3145728]{0:T(1024)(128)(4,1)S(1)}, s32[]{:S(2)}) async-start(s8[7340032]{0:T(1024)(128)(4,1)} %bitcast.144), calls=%async_computation.11 | async-start | bytes 6291456
  255.0 52.7 %all-to-all-start.3 = ((bf16[16,256,1,1,448]{1,4,3,2,0:T(8,128)(2,1)}), bf16[16,256,1,1,448]{1,4,3,2,0:T(8,128)(2,1)}, u32[]{:S(2)}, u32[]{:S(2)}) async-start(bf16[16,256,1,1,448]{1,4,3,2,0:T(8,128)(2,1)} %fusion.266), calls=%async_computation.3 | async-start | bytes 7340032 | tf_op jit(solution)/shard_map/all_to_all | solution.py:76
  307.7 87.5 %all-to-all-start.5 = ((bf16[8,2,2,16,2,3584]{5,4,3,2,1,0:T(2,128)(2,1)}), bf16[8,2,2,16,2,3584]{5,4,3,2,1,0:T(2,128)(2,1)}, u32[]{:S(2)}, u32[]{:S(2)}) async-start(bf16[8,2,2,16,2,3584]{5,4,3,2,1,0:T(2,128)(2,1)} %copy.44), calls=%async_computation.5 | async-start | bytes 14680064 | tf_op jit(solution)/shard_map/all_to_all | solution.py:103
